TPU v7x, 128 devices: a whole 4x4x4 slice. The times are simulated.
128 devices in a mesh: row: 8 (over y, core), col: 16 (over z, x).
Axes of the slice: x: 4, y: 4, z: 4, core: 2. Of those that a mesh axis runs over, the one named last changes fastest.
Arguments:
- features: float32 [256, 1024, 128], P('row', 'col'), may hold values from -0.4 to 0.4
- step_size: float32 [256, 1024, 128], P('row', 'col'), may hold values from 0.5 to 2
- write_weights: float32 [256, 1024, 16], P('row', 'col'), may hold values from -6 to 6
- read_weights: float32 [256, 1024, 16], P('row', 'col'), may hold values from -6 to 6
- decay_log: float32 [16, 128], replicated, may hold values from -7.6 to -3.5
- out_grad: float32 [256, 1024, 128], P('row', 'col'), may hold values from -0.4 to 0.4
Outputs:
- grad_features: float32 [256, 1024, 128], P('row', 'col')
- grad_step: float32 [256, 1024, 128], P('row', 'col')
- grad_write: float32 [256, 1024, 16], P('row', 'col')
- grad_read: float32 [256, 1024, 16], P('row', 'col')
- grad_decay: float32 [16, 128], replicated
All inputs are finite; a program needn't handle non-finite values.
Results may differ from a plain program's by a relative error of at most 0.0002.
Values sent between devices are 32-bit elements; how exact they have to be, the bound alone decides.
A program may use at most 320 MiB of HBM per device.

v0:
```python
import jax
import jax.numpy as jnp
from jax import lax
from jax.sharding import PartitionSpec as P


def carried_in(shard, axis, combine, identity, reverse):
    size, mine = (lax.axis_size(axis), lax.axis_index(axis))
    everything = jax.tree.map(lambda part: lax.all_gather(part, axis), shard)
    start = jax.tree.map(
        lambda part, zero: jnp.broadcast_to(jnp.asarray(zero, part.dtype), part.shape),
        shard,
        identity,
    )

    def lap(k, before):
        at = size - 1 - k if reverse else k
        reached = at > mine if reverse else at < mine
        new = combine(before, jax.tree.map(lambda part: part[at], everything))
        return jax.tree.map(lambda a, b: jnp.where(reached, a, b), new, before)

    return lax.fori_loop(0, size, lap, start)


def sweep_rows(decays, driving, backward):

    def advance(current, inputs):
        factor, source = inputs
        current = factor * current + source
        return (current, current)

    def retreat(passed, inputs):
        factor, source = inputs
        adjoint = source + passed
        return (factor * adjoint, adjoint)

    initial = jnp.zeros(decays.shape[1:], jnp.float32)
    if backward:
        closing, values = lax.scan(retreat, initial, (decays, driving), reverse=True)
    else:
        closing, values = lax.scan(advance, initial, (decays, driving))
    return (values, closing)


def sweep_cols(decays, driving, backward):
    length = decays.shape[1]

    def advance(index, running):
        current, values = running
        place = length - 1 - index if backward else index
        place = jnp.asarray(place).astype(jnp.int32)
        factor = lax.dynamic_index_in_dim(decays, place, 1, keepdims=False)
        source = lax.dynamic_index_in_dim(driving, place, 1, keepdims=False)
        if backward:
            value = source + current
            values = lax.dynamic_update_index_in_dim(values, value, place, 1)
            current = factor * value
        else:
            current = factor * current + source
            values = lax.dynamic_update_index_in_dim(values, current, place, 1)
        return (current, values)

    initial = jnp.zeros(decays.shape[:1] + decays.shape[2:], jnp.float32)
    closing, values = lax.fori_loop(0, length, advance, (initial, jnp.zeros_like(driving)))
    return (values, closing)


def link_parts(final_state, exponent_sum, decay_rate):

    def combine(earlier, subsequent):
        return (earlier[0] * subsequent[0], subsequent[0] * earlier[1] + subsequent[1])

    products = jnp.exp(exponent_sum[:, None, :] * decay_rate)
    element = (products, final_state)
    identity = (jnp.ones_like(products), jnp.zeros_like(final_state))
    return (element, identity, combine)


def shards(features, step_size, write_weights, read_weights, decay_log, out_grad):
    highest = lax.Precision.HIGHEST
    decay_rate = -jnp.exp(decay_log)
    decays = jnp.exp(step_size[:, :, None, :] * decay_rate)
    driving = step_size[:, :, None, :] * write_weights[:, :, :, None] * features[:, :, None, :]
    running_rows = jnp.cumsum(step_size, 0)
    running_cols = jnp.cumsum(step_size, 1)
    sum_rows = running_rows[-1]
    sum_cols = running_cols[:, -1]
    local_rows, leaving_rows = sweep_rows(decays, driving, False)
    element, identity, combine = link_parts(leaving_rows, sum_rows, decay_rate)
    from_above = carried_in(element, "row", combine, identity, False)[1]
    vertical = local_rows + jnp.exp(running_rows[:, :, None, :] * decay_rate) * from_above[None]
    vert_prev = jnp.concatenate([from_above[None], vertical[:-1]], 0)
    local_cols, leaving_cols = sweep_cols(decays, vertical, False)
    element, identity, combine = link_parts(leaving_cols, sum_cols, decay_rate)
    from_left = carried_in(element, "col", combine, identity, False)[1]
    states = local_cols + jnp.exp(running_cols[:, :, None, :] * decay_rate) * from_left[:, None]
    states_prev = jnp.concatenate([from_left[:, None], states[:, :-1]], 1)
    direct = read_weights[:, :, :, None] * out_grad[:, :, None, :]
    adjoint_local, outgoing_cols = sweep_cols(decays, direct, True)
    element, identity, combine = link_parts(outgoing_cols, sum_cols, decay_rate)
    from_right = carried_in(element, "col", combine, identity, True)[1]
    after_cols = sum_cols[:, None, :] - running_cols
    adjoint_h = (
        adjoint_local + jnp.exp(after_cols[:, :, None, :] * decay_rate) * from_right[:, None]
    )
    adjoint_vlocal, outgoing_rows = sweep_rows(decays, adjoint_h, True)
    element, identity, combine = link_parts(outgoing_rows, sum_rows, decay_rate)
    from_below = carried_in(element, "row", combine, identity, True)[1]
    after_rows = sum_rows[None] - running_rows
    adjoint_v = adjoint_vlocal + jnp.exp(after_rows[:, :, None, :] * decay_rate) * from_below[None]
    exponent_grad = (adjoint_h * states_prev + adjoint_v * vert_prev) * decays
    through = jnp.einsum("hwnd,hwn->hwd", adjoint_v, write_weights, precision=highest)
    grad_features = step_size * through
    grad_step = features * through + jnp.einsum(
        "hwnd,nd->hwd", exponent_grad, decay_rate, precision=highest
    )
    grad_write = jnp.einsum("hwnd,hwd->hwn", adjoint_v, step_size * features, precision=highest)
    grad_read = jnp.einsum("hwnd,hwd->hwn", states, out_grad, precision=highest)
    partial_sum = jnp.einsum("hwnd,hwd->nd", exponent_grad, step_size, precision=highest)
    grad_decay = lax.psum(partial_sum, ("row", "col")) * decay_rate
    return (grad_features, grad_step, grad_write, grad_read, grad_decay)


def solution(mesh):
    in_specs = (
        P("row", "col", None),
        P("row", "col", None),
        P("row", "col", None),
        P("row", "col", None),
        P(),
        P("row", "col", None),
    )
    out_specs = (
        P("row", "col", None),
        P("row", "col", None),
        P("row", "col", None),
        P("row", "col", None),
        P(),
    )
    return jax.shard_map(shards, mesh=mesh, in_specs=in_specs, out_specs=out_specs, check_vma=False)
```

profile of v0, /device:TPU:1, one launch (start us, length us, event | category | flops | bytes accessed | tf_op | source)
XLA Modules:
  0.0 968.1 jit_solution(15481916507911445551)
XLA Ops:
  13.7 9.3 multiply_multiply_fusion
  23.0 5.8 copy-done
  28.8 6.2 copy.32
  35.0 7.9 broadcast.59.clone3
  42.9 79.4 %while.128 = (s32[]{:T(128)}, f32[64,16,128]{2,1,0:T(8,128)S(1)}, f32[32,64,16,128]{3,2,0,1:T(8,128)}, f32[32,64,16,128]{3,2,1,0:T(8,128)}, f32[32,64,16,128]{3,2,0,1:T(8,128)}, /*index=5*/s32[]{:T(128)}, s32[]{:T(128)}) while((s32[]{:T(128)}, f32[64,16,128]{2,1,0:T(8,128)S(1)}, f32[32,64,16,128]{3,2,0,1:T(8,128)}, ...), condition=%wide.region_11.12_spmd.clone, body=%wide.region_10.11_spmd.clone.sunk | while | flops 393219 | bytes 2622039 | solution.py:41
  42.9 2.5 bitcast_dynamic-update-slice_fusion.10
  45.4 2.5 bitcast_dynamic-update-slice_fusion.10
  47.9 2.5 bitcast_dynamic-update-slice_fusion.10
  50.4 2.5 bitcast_dynamic-update-slice_fusion.10
  52.9 2.5 bitcast_dynamic-update-slice_fusion.10
  55.4 2.5 bitcast_dynamic-update-slice_fusion.10
  57.9 2.5 bitcast_dynamic-update-slice_fusion.10
  60.4 2.5 bitcast_dynamic-update-slice_fusion.10
  62.8 2.5 bitcast_dynamic-update-slice_fusion.10
  65.3 2.5 bitcast_dynamic-update-slice_fusion.10
  67.8 2.5 bitcast_dynamic-update-slice_fusion.10
  70.3 2.5 bitcast_dynamic-update-slice_fusion.10
  72.8 2.5 bitcast_dynamic-update-slice_fusion.10
  75.2 2.5 bitcast_dynamic-update-slice_fusion.10
  77.7 2.5 bitcast_dynamic-update-slice_fusion.10
  80.2 2.5 bitcast_dynamic-update-slice_fusion.10
  82.6 2.5 bitcast_dynamic-update-slice_fusion.10
  85.1 2.5 bitcast_dynamic-update-slice_fusion.10
  87.6 2.5 bitcast_dynamic-update-slice_fusion.10
  90.1 2.5 bitcast_dynamic-update-slice_fusion.10
  92.6 2.5 bitcast_dynamic-update-slice_fusion.10
  95.0 2.5 bitcast_dynamic-update-slice_fusion.10
  97.5 2.5 bitcast_dynamic-update-slice_fusion.10
  100.1 2.5 bitcast_dynamic-update-slice_fusion.10
  102.5 2.5 bitcast_dynamic-update-slice_fusion.10
  105.0 2.5 bitcast_dynamic-update-slice_fusion.10
  107.4 2.5 bitcast_dynamic-update-slice_fusion.10
  109.9 2.5 bitcast_dynamic-update-slice_fusion.10
  112.4 2.5 bitcast_dynamic-update-slice_fusion.10
  114.8 2.5 bitcast_dynamic-update-slice_fusion.10
  117.3 2.5 bitcast_dynamic-update-slice_fusion.10
  119.8 2.5 bitcast_dynamic-update-slice_fusion.10
  123.2 4.0 fusion.18
  134.2 7.6 broadcast_multiply_fusion
  141.8 8.0 broadcast.59.clone3.2
  149.7 186.2 %while.124 = (s32[]{:T(128)}, f32[32,16,128]{2,1,0:T(8,128)S(1)}, f32[32,64,16,128]{3,2,0,1:T(8,128)}, f32[32,64,16,128]{3,2,0,1:T(8,128)}, f32[32,64,16,128]{3,...) while((s32[]{:T(128)}, f32[32,16,128]{2,1,0:T(8,128)S(1)}, ...), condition=%wide.region_1.2_spmd.clone, body=%wide.region_0.0_spmd.clone.sunk | while | flops 327687 | bytes 1835166 | solution.py:64
  338.5 13.5 %while.129 = (s32[]{:T(128)}, f32[64,16,128]{2,1,0:T(8,128)S(1)}, s32[]{:T(128)}, f32[8,64,16,128]{3,2,1,0:T(8,128)}, f32[8,64,16,128]{3,2,1,0:T(8,128)}, /*index=5*/s32[]{:T(128)}, s32[]{:T(128)}) while((s32[]{:T(128)}, f32[64,16,128]{2,1,0:T(8,128)S(1)}, s32[]{:T(128)}, f32[8,64,16,128]{3,2,1,0:T(8,128)}, ...), condition=%wide.region_13.14_spmd.clone, body=%wide.region_12.13_spmd.clone.sunk | while | flops 524292 | bytes 2097253 | solution.py:22
  352.0 12.2 %multiply_add_fusion.1 = f32[32,64,16,128]{3,2,0,1:T(8,128)} fusion(f32[32,64,16,128]{3,2,0,1:T(8,128)} %get-tuple-element.823, f32[64,16,128]{2,1,0:T(8,128)S(1)} %get-tuple-element.825, f32[32,64,128]{2,0,1:T(8,128)} %copy.41, f32[16,128]{1,0:T(8,128)S(1)} %exponential_negate_fusion), kind=kLoop, calls=%fused_computation.33 | loop fusion | flops 12582912 | bytes 35135488 | tf_op jit(solution)/shard_map/add | solution.py:91
  364.2 8.0 broadcast.59.clone3.1
  372.2 124.9 %while.130 = (s32[]{:T(128)}, f32[32,16,128]{2,1,0:T(8,128)S(1)}, f32[32,64,16,128]{3,2,0,1:T(8,128)}, f32[32,64,16,128]{3,2,0,1:T(8,128)}, f32[32,64,16,128]{3,2,0,1:T(8,128)}, /*index=5*/s32[]{:T(128)}, s32[]{:T(128)}) while((s32[]{:T(128)}, f32[32,16,128]{2,1,0:T(8,128)S(1)}, f32[32,64,16,128]{3,2,0,1:T(8,128)}, ...), condition=%wide.region_15.16_spmd.clone, body=%wide.region_14.15_spmd.clone.sunk | while | flops 196611 | bytes 1311319 | solution.py:64
  497.9 2.3 broadcast_subtract_fusion.1
  500.2 29.8 %while.125 = (s32[]{:T(128)}, f32[32,16,128]{2,1,0:T(8,128)}, s32[]{:T(128)}, f32[16,32,16,128]{3,2,1,0:T(8,128)}, f32[16,32,16,128]{3,2,1,0:T(8,128)}, /*index=5*/s32[]{:T(128)}, s32[]{:T(128)}, s32[]{:T(128)}, s32[]{:T(128)}) while((s32[]{:T(128)}, f32[32,16,128]{2,1,0:T(8,128)}, s32[]{:T(128)}, f32[16,32,16,128]{3,2,1,0:T(8,128)}, ...), condition=%wide.region_4.5_spmd.clone, body=%wide.region_3.4_spmd.clone.sunk | while | flops 262152 | bytes 1048739 | solution.py:22
  530.0 22.9 %all-gather.21.cloned.1.call-done = f32[512,16,128]{2,1,0:T(8,128)} async-done(((f32[32,16,128]{2,1,0:T(8,128)}), f32[512,16,128]{2,1,0:T(8,128)}) %all-gather.21.cloned.1.call-update) | async-done | bytes 4194320 | tf_op jit(solution)/shard_map/all_gather | solution.py:9
  552.9 20.3 %while.131 = (s32[]{:T(128)}, f32[32,16,128]{2,1,0:T(8,128)S(1)}, s32[]{:T(128)}, f32[16,32,16,128]{3,2,1,0:T(8,128)}, f32[16,32,16,128]{3,2,1,0:T(8,128)}, /*index=5*/s32[]{:T(128)}, s32[]{:T(128)}) while((s32[]{:T(128)}, f32[32,16,128]{2,1,0:T(8,128)S(1)}, s32[]{:T(128)}, f32[16,32,16,128]{3,2,1,0:T(8,128)}, ...), condition=%wide.region_17.18_spmd.clone, body=%wide.region_16.17_spmd.clone.sunk | while | flops 262148 | bytes 1048677 | solution.py:22
  573.2 23.2 %multiply_add_fusion = (f32[32,64,16,128]{3,2,0,1:T(8,128)}, f32[32,64,16,128]{3,2,0,1:T(8,128)}) fusion(f32[32,64,16,128]{3,2,0,1:T(8,128)} %get-tuple-element.828, f32[32,16,128]{2,1,0:T(8,128)S(1)} %get-tuple-element.827, f32[32,64,128]{2,0,1:T(8,128)} %copy-done.5, f32[16,128]{1,0:T(8,128)S(1)} %exponential_negate_fusion, ...), kind=kLoop, calls=%fused_computation.32 | loop fusion | flops 25165824 | bytes 69738496 | tf_op jit(solution)/shard_map/add | solution.py:96
  596.4 7.9 broadcast.59.clone2
  604.3 113.4 %while.126 = (s32[]{:T(128)}, f32[64,16,128]{2,1,0:T(8,128)S(1)}, f32[32,64,16,128]{3,2,0,1:T(8,128)}, f32[32,64,16,128]{3,2,1,0:T(8,128)}, f32[32,64,16,128]{3,...) while((s32[]{:T(128)}, f32[64,16,128]{2,1,0:T(8,128)S(1)}, f32[32,64,16,128]{3,2,0,1:T(8,128)}, ...), condition=%wide.region_6.7_spmd.clone, body=%wide.region_5.6_spmd.clone.sunk | while | flops 655364 | bytes 3670132 | solution.py:39
  721.8 2.9 copy.44
  724.7 11.6 %slice.19 = f32[31,64,16,128]{3,2,0,1:T(8,128)} slice(f32[32,64,16,128]{3,2,0,1:T(8,128)} %get-tuple-element.1542), slice={[0:31], [0:64], [0:16], [0:128]} | slice | bytes 32505856 | tf_op jit(solution)/shard_map/slice | solution.py:92
  736.3 13.9 %slice.18 = f32[32,63,16,128]{3,2,0,1:T(8,128)} slice(f32[32,64,16,128]{3,2,0,1:T(8,128)} %get-tuple-element.1087), slice={[0:32], [0:63], [0:16], [0:128]} | slice | bytes 33030144 | tf_op jit(solution)/shard_map/slice | solution.py:97
  753.5 27.6 %fusion.6 = f32[32,64,1,16]{3,2,1,0:T(1,128)} fusion(f32[32,64,128,1]{2,3,1,0:T(1,128)S(1)} %bitcast.158, f32[32,64,16,128]{3,2,0,1:T(8,128)S(1)} %bitcast.152), kind=kOutput, calls=%fused_computation.29 | convolution fusion | flops 50331648 | bytes 17956864 | tf_op jit(solution)/shard_map/hwnd,hwd->hwn/dot_general | solution.py:118
  781.1 2.9 copy.57
  784.1 13.5 %while.127 = (s32[]{:T(128)}, f32[64,16,128]{2,1,0:T(8,128)S(1)}, s32[]{:T(128)}, f32[8,64,16,128]{3,2,1,0:T(8,128)}, f32[8,64,16,128]{3,2,1,0:T(8,128)}, /*index=5*/s32[]{:T(128)}, s32[]{:T(128)}, s32[]{:T(128)}, s32[]{:T(128)}) while((s32[]{:T(128)}, f32[64,16,128]{2,1,0:T(8,128)S(1)}, s32[]{:T(128)}, ...), condition=%wide.region_9.10_spmd.clone, body=%wide.region_8.9_spmd.clone.sunk | while | flops 524296 | bytes 2097315 | solution.py:22
  797.6 34.8 %multiply_reduce_fusion = (f32[128,16]{0,1:T(8,128)S(1)}, f32[32,64,16,128]{3,2,0,1:T(8,128)}, f32[32,64,16,128]{3,2,0,1:T(8,128)}) fusion(f32[128,32,64]{0,1,2:T(8,128)} %copy.74, f32[16,128]{1,0:T(8,128)S(1)} %exponential_negate_fusion, f32[32,64,128]{2,0,1:T(8,128)S(1)} %copy-done.7, f32[31,64,16,128]{3,2,0,1:T(8,128)} %slice.19, ...), kind=kLoop, calls=%fused_computation.28 | loop fusion | flops 50329600 | bytes 104349696 | tf_op jit(solution)/shard_map/hwnd,hwd->nd/dot_general | solution.py:119
  832.3 64.6 %psum.7 = f32[16,128]{1,0:T(8,128)S(1)} all-reduce(f32[16,128]{1,0:T(8,128)S(1)} %bitcast.166), channel_id=1, replica_groups=mesh['row'=8,'col'=16] {'row','col'}, use_global_device_ids=true, to_apply=%region_18.19 | all-reduce | flops 2048 | bytes 16384 | tf_op jit(solution)/shard_map/psum | solution.py:120
  897.5 18.2 %fusion.10 = f32[32,64,1,128]{3,2,1,0:T(1,128)S(1)} fusion(f32[32,64,16,1]{2,3,1,0:T(1,128)} %copy.44, f32[32,64,16,128]{3,2,0,1:T(8,128)} %get-tuple-element.1079), kind=kOutput, calls=%fused_computation.40 | convolution fusion | flops 50331648 | bytes 17956864 | tf_op jit(solution)/shard_map/hwnd,hwn->hwd/dot_general | solution.py:112
  915.7 10.9 %multiply_reduce_fusion.1 = f32[128,32,64]{0,1,2:T(8,128)} fusion(f32[32,64,16,128]{3,2,0,1:T(8,128)} %get-tuple-element.1078, f32[128,16]{0,1:T(8,128)S(1)} %get-tuple-element.1086), kind=kLoop, calls=%fused_computation.31 | loop fusion | flops 8126464 | bytes 17833984
  926.6 3.6 fusion.17
  930.2 28.9 %fusion.8 = f32[32,64,1,16]{3,2,1,0:T(1,128)S(1)} fusion(f32[32,64,128,1]{2,3,1,0:T(1,128)S(1)} %bitcast.157, f32[32,64,16,128]{3,2,0,1:T(8,128)} %get-tuple-element.1079), kind=kOutput, calls=%fused_computation.38 | convolution fusion | flops 50331648 | bytes 17956864 | tf_op jit(solution)/shard_map/hwnd,hwd->hwn/dot_general | solution.py:117
  (378 shorter events, 526.2 us)
Async XLA Ops:
  7.2 331.3 %all-gather.19.cloned.1.call-start = ((), (), s32[]{:S(2)}) async-start(), calls=%async_computation.4 | async-start | bytes 4718592 | tf_op jit(solution)/shard_map/all_gather | solution.py:9
  9.8 13.2 %copy-start.6 = (f32[32,64,128]{2,0,1:T(8,128)}, f32[32,64,128]{2,0,1:T(8,128)S(1)}, u32[]{:S(2)}) copy-start(f32[32,64,128]{2,0,1:T(8,128)S(1)} %copy.27) | copy-start | bytes 3145732
  23.0 5.8 copy-start
  35.0 88.2 %copy-start.3 = (f32[32,64,128]{2,1,0:T(8,128)S(1)}, f32[32,64,128]{2,1,0:T(8,128)}, u32[]{:S(2)}) copy-start(f32[32,64,128]{2,1,0:T(8,128)} %param.23) | copy-start | bytes 3145732
  35.0 95.6 %copy-start.10 = (f32[32,64,16]{1,2,0:T(8,128)S(1)}, f32[32,64,16]{1,2,0:T(8,128)}, u32[]{:S(2)}) copy-start(f32[32,64,16]{1,2,0:T(8,128)} %param.25) | copy-start | bytes 393220
  122.3 0.8 copy-start.4
  123.1 215.4 %all-gather.13.cloned.1.call-start = ((), (), s32[]{:S(2)}) async-start(), calls=%async_computation.1 | async-start | bytes 4718592 | tf_op jit(solution)/shard_map/all_gather | solution.py:9
  128.1 372.1 %all-gather.11.cloned.1.call-start = ((), (), s32[]{:S(2)}) async-start(), calls=%async_computation | async-start | bytes 4456448 | tf_op jit(solution)/shard_map/all_gather | solution.py:9
  128.7 1.0 copy-start.5
  130.5 369.7 %all-gather.15.cloned.1.call-start = ((), (), s32[]{:S(2)}) async-start(), calls=%async_computation.2 | async-start | bytes 4456448 | tf_op jit(solution)/shard_map/all_gather | solution.py:9
  336.0 0.7 copy-start.2
  336.7 216.2 %all-gather.21.cloned.1.call-start = ((), (), s32[]{:S(2)}) async-start(), calls=%async_computation.5 | async-start | bytes 4456448 | tf_op jit(solution)/shard_map/all_gather | solution.py:9
  497.1 0.7 copy-start.8
  497.8 286.3 %all-gather.17.cloned.1.call-start = ((), (), s32[]{:S(2)}) async-start(), calls=%async_computation.3 | async-start | bytes 4718592 | tf_op jit(solution)/shard_map/all_gather | solution.py:9
  717.7 0.8 copy-start.1
  736.2 14.0 %slice-start = ((s8[16777216]{0:T(1024)(128)(4,1)}), s8[4194304]{0:T(1024)(128)(4,1)S(1)}, s32[]{:S(2)}) async-start(s8[16777216]{0:T(1024)(128)(4,1)} %bitcast.151), calls=%async_computation.6 | async-start | bytes 8388608
  736.2 14.0 %copy-start.9 = (f32[32,64,128]{2,1,0:T(8,128)S(1)}, f32[32,64,128]{2,1,0:T(8,128)}, u32[]{:S(2)}) copy-start(f32[32,64,128]{2,1,0:T(8,128)} %param.27) | copy-start | bytes 3145732
  736.2 14.6 %slice-start.1 = ((s8[16777216]{0:T(1024)(128)(4,1)}), s8[4194304]{0:T(1024)(128)(4,1)S(1)}, s32[]{:S(2)}) async-start(s8[16777216]{0:T(1024)(128)(4,1)} %bitcast.151), calls=%async_computation.7 | async-start | bytes 8388608
  736.3 16.1 %slice-start.2 = ((s8[16777216]{0:T(1024)(128)(4,1)}), s8[4194304]{0:T(1024)(128)(4,1)S(1)}, s32[]{:S(2)}) async-start(s8[16777216]{0:T(1024)(128)(4,1)} %bitcast.151), calls=%async_computation.8 | async-start | bytes 8388608
  736.3 17.2 %slice-start.3 = ((s8[16777216]{0:T(1024)(128)(4,1)}), s8[4194304]{0:T(1024)(128)(4,1)S(1)}, s32[]{:S(2)}) async-start(s8[16777216]{0:T(1024)(128)(4,1)} %bitcast.151), calls=%async_computation.9 | async-start | bytes 8388608
  753.5 44.0 %copy-start.7 = (f32[32,64,128]{2,0,1:T(8,128)S(1)}, f32[32,64,128]{2,0,1:T(8,128)}, u32[]{:S(2)}) copy-start(f32[32,64,128]{2,0,1:T(8,128)} %copy-done.6) | copy-start | bytes 3145732
  797.6 99.3 %copy-start.11 = (f32[16,128]{1,0:T(8,128)S(1)}, f32[16,128]{1,0:T(8,128)}, u32[]{:S(2)}) copy-start(f32[16,128]{1,0:T(8,128)} %param.26) | copy-start | bytes 24580
Sparse Core Ops, SparseCore 0:
  123.2 35.7 all-gather.18
  160.7 32.0 all-gather.12
  195.6 51.1 all-gather.10
  336.8 54.8 all-gather.14
  497.9 54.8 all-gather.20
  718.6 32.1 all-gather.16
where the time goes:
time: 984 us; the launch traced here: 968 us
  other arithmetic  690 us (70%)
  local copies, waits for them, and re-layouts  98.4 us (10%)
  matrix products  74.7 us (8%)
  blocking collectives  64.6 us (7%)
  waiting for transfers between devices  23 us (2%)
  between operations  14.6 us (1%)
    dynamic_update_slice x64, other arithmetic, sweep_rows(): closing, values = lax.scan(advance, initial, (decays, driving))  143 us
    dynamic_update_slice x64, other arithmetic, advance(): values = lax.dynamic_update_index_in_dim(values, current, place, 1)  125 us
    dynamic_update_slice x64, other arithmetic, advance(): values = lax.dynamic_update_index_in_dim(values, value, place, 1)  108 us
    mul x64, other arithmetic, advance(): current = factor * value  76.4 us
    select_n x48, other arithmetic, lap(): return jax.tree.map(lambda a, b: jnp.where(reached, a, b), new, before)  76.4 us
    psum x1, blocking collectives, shards(): grad_decay = lax.psum(partial_sum, ('row', 'col')) * decay_rate  64.6 us
    mul x32, other arithmetic, retreat(): return (factor * adjoint, adjoint)  49.2 us
    dot_general x1, other arithmetic, shards(): jnp.einsum('hwnd,hwd->nd', exponent_grad, step_size, precision=highest)  34.8 us
  transfers between devices with their start and end apart: 6, of which 1 were waited for; matrix products, arithmetic and copies ran while one was open for 48% of the time, Pallas kernels for 0%

commit v1 on v0

--- a/solution.py
+++ b/solution.py
@@ -77,6 +77,10 @@
 
 
 def shards(features, step_size, write_weights, read_weights, decay_log, out_grad):
+
+    def paths_direct(z, mesh_dim):
+        return jnp.sum(jax.lax.all_gather(z, mesh_dim), axis=0)
+
     highest = lax.Precision.HIGHEST
     decay_rate = -jnp.exp(decay_log)
     decays = jnp.exp(step_size[:, :, None, :] * decay_rate)
@@ -117,7 +121,7 @@
     grad_write = jnp.einsum("hwnd,hwd->hwn", adjoint_v, step_size * features, precision=highest)
     grad_read = jnp.einsum("hwnd,hwd->hwn", states, out_grad, precision=highest)
     partial_sum = jnp.einsum("hwnd,hwd->nd", exponent_grad, step_size, precision=highest)
-    grad_decay = lax.psum(partial_sum, ("row", "col")) * decay_rate
+    grad_decay = paths_direct(partial_sum, ("row", "col")) * decay_rate
     return (grad_features, grad_step, grad_write, grad_read, grad_decay)
 
 

time: 984 us -> 933 us (0.948)
  blocking collectives: 64.6 us -> 0 us
  waiting for transfers between devices: 23 us -> 41.7 us
    psum x1 -> x0, blocking collectives: 64.6 us -> none  [shards(): grad_decay = lax.psum(partial_sum, ('row', 'col')) * decay_rate]
    all_gather x0 -> x1, waiting for transfers between devices: none -> 11.6 us  [paths_direct(): return jnp.sum(jax.lax.all_gather(z, mesh_dim), axis=0)]
    unnamed x40 -> x38, local copies, waits for them, and re-layouts: 33.1 us -> 32.1 us
  transfers between devices with their start and end apart: 6 -> 7, of which waited for: 1 -> 3; matrix products, arithmetic and copies ran while one was open for 48% -> 52% of each run, Pallas kernels for 0% -> 0%
where the time goes in v1:
time: 933 us; the launch traced here: 917 us
  other arithmetic  691 us (74%)
  local copies, waits for them, and re-layouts  90.2 us (10%)
  matrix products  76.1 us (8%)
  waiting for transfers between devices  41.7 us (4%)
  between operations  14.8 us (2%)
    dynamic_update_slice x64, other arithmetic, sweep_rows(): closing, values = lax.scan(advance, initial, (decays, driving))  141 us
    dynamic_update_slice x64, other arithmetic, advance(): values = lax.dynamic_update_index_in_dim(values, current, place, 1)  125 us
    dynamic_update_slice x64, other arithmetic, advance(): values = lax.dynamic_update_index_in_dim(values, value, place, 1)  109 us
    select_n x48, other arithmetic, lap(): return jax.tree.map(lambda a, b: jnp.where(reached, a, b), new, before)  76.4 us
    mul x64, other arithmetic, advance(): current = factor * value  76.3 us
    mul x32, other arithmetic, retreat(): return (factor * adjoint, adjoint)  49.2 us
    dot_general x1, other arithmetic, shards(): jnp.einsum('hwnd,hwd->nd', exponent_grad, step_size, precision=highest)  35.4 us
    unnamed x38, local copies, waits for them, and re-layouts  32.1 us
  transfers between devices with their start and end apart: 7, of which 3 were waited for; matrix products, arithmetic and copies ran while one was open for 52% of the time, Pallas kernels for 0%

profile of v1, /device:TPU:1, one launch (start us, length us, event | category | flops | bytes accessed | tf_op | source)
XLA Modules:
  0.0 917.2 jit_solution(5525591677716512331)
XLA Ops:
  13.7 9.3 %multiply_multiply_fusion = (f32[32,64,16,128]{3,2,0,1:T(8,128)}, f32[32,64,16,128]{3,2,0,1:T(8,128)S(1)}) fusion(f32[32,64,128]{2,0,1:T(8,128)S(1)} %copy.53, f32[32,64,16]{2,0,1:T(8,128)S(1)} %copy.52, f32[32,64,128]{2,0,1:T(8,128)S(1)} %copy.43, f32[16,128]{1,0:T(8,128)S(1)} %exponential_negate_fusion), kind=kLoop, calls=%fused_computation.34 | loop fusion | flops 12582912 | bytes 35790848 | tf_op jit(solution)/shard_map/mul | solution.py:87
  23.0 5.7 copy-done
  28.8 6.2 copy.48
  34.9 7.8 broadcast.59.clone3
  42.7 79.3 %while.128 = (s32[]{:T(128)}, f32[64,16,128]{2,1,0:T(8,128)S(1)}, f32[32,64,16,128]{3,2,0,1:T(8,128)}, f32[32,64,16,128]{3,2,1,0:T(8,128)}, f32[32,64,16,128]{3,2,0,1:T(8,128)}, /*index=5*/s32[]{:T(128)}, s32[]{:T(128)}) while((s32[]{:T(128)}, f32[64,16,128]{2,1,0:T(8,128)S(1)}, f32[32,64,16,128]{3,2,0,1:T(8,128)}, ...), condition=%wide.region_11.12_spmd.clone, body=%wide.region_10.11_spmd.clone.sunk | while | flops 393219 | bytes 2622039 | solution.py:41
  42.7 2.5 bitcast_dynamic-update-slice_fusion.10
  45.3 2.5 bitcast_dynamic-update-slice_fusion.10
  47.8 2.5 bitcast_dynamic-update-slice_fusion.10
  50.2 2.5 bitcast_dynamic-update-slice_fusion.10
  52.7 2.5 bitcast_dynamic-update-slice_fusion.10
  55.2 2.5 bitcast_dynamic-update-slice_fusion.10
  57.7 2.5 bitcast_dynamic-update-slice_fusion.10
  60.2 2.5 bitcast_dynamic-update-slice_fusion.10
  62.6 2.5 bitcast_dynamic-update-slice_fusion.10
  65.1 2.5 bitcast_dynamic-update-slice_fusion.10
  67.6 2.5 bitcast_dynamic-update-slice_fusion.10
  70.0 2.5 bitcast_dynamic-update-slice_fusion.10
  72.5 2.5 bitcast_dynamic-update-slice_fusion.10
  75.0 2.5 bitcast_dynamic-update-slice_fusion.10
  77.5 2.5 bitcast_dynamic-update-slice_fusion.10
  80.0 2.5 bitcast_dynamic-update-slice_fusion.10
  82.5 2.5 bitcast_dynamic-update-slice_fusion.10
  85.0 2.5 bitcast_dynamic-update-slice_fusion.10
  87.5 2.5 bitcast_dynamic-update-slice_fusion.10
  90.0 2.5 bitcast_dynamic-update-slice_fusion.10
  92.4 2.5 bitcast_dynamic-update-slice_fusion.10
  94.9 2.5 bitcast_dynamic-update-slice_fusion.10
  97.4 2.4 bitcast_dynamic-update-slice_fusion.10
  99.8 2.5 bitcast_dynamic-update-slice_fusion.10
  102.3 2.4 bitcast_dynamic-update-slice_fusion.10
  104.7 2.4 bitcast_dynamic-update-slice_fusion.10
  107.2 2.5 bitcast_dynamic-update-slice_fusion.10
  109.6 2.5 bitcast_dynamic-update-slice_fusion.10
  112.1 2.5 bitcast_dynamic-update-slice_fusion.10
  114.6 2.5 bitcast_dynamic-update-slice_fusion.10
  117.0 2.5 bitcast_dynamic-update-slice_fusion.10
  119.5 2.5 bitcast_dynamic-update-slice_fusion.10
  122.9 4.0 fusion.18
  133.9 7.5 broadcast_multiply_fusion
  141.4 8.0 broadcast.59.clone3.2
  149.4 186.5 %while.124 = (s32[]{:T(128)}, f32[32,16,128]{2,1,0:T(8,128)S(1)}, f32[32,64,16,128]{3,2,0,1:T(8,128)}, f32[32,64,16,128]{3,2,0,1:T(8,128)}, f32[32,64,16,128]{3,...) while((s32[]{:T(128)}, f32[32,16,128]{2,1,0:T(8,128)S(1)}, ...), condition=%wide.region_1.2_spmd.clone, body=%wide.region_0.0_spmd.clone.sunk | while | flops 327687 | bytes 1835166 | solution.py:64
  338.8 13.5 %while.129 = (s32[]{:T(128)}, f32[64,16,128]{2,1,0:T(8,128)S(1)}, s32[]{:T(128)}, f32[8,64,16,128]{3,2,1,0:T(8,128)}, f32[8,64,16,128]{3,2,1,0:T(8,128)}, /*index=5*/s32[]{:T(128)}, s32[]{:T(128)}) while((s32[]{:T(128)}, f32[64,16,128]{2,1,0:T(8,128)S(1)}, s32[]{:T(128)}, f32[8,64,16,128]{3,2,1,0:T(8,128)}, ...), condition=%wide.region_13.14_spmd.clone, body=%wide.region_12.13_spmd.clone.sunk | while | flops 524292 | bytes 2097253 | solution.py:22
  352.3 12.2 %multiply_add_fusion.1 = f32[32,64,16,128]{3,2,0,1:T(8,128)} fusion(f32[32,64,16,128]{3,2,0,1:T(8,128)} %get-tuple-element.823, f32[64,16,128]{2,1,0:T(8,128)S(1)} %get-tuple-element.825, f32[32,64,128]{2,0,1:T(8,128)} %copy.57, f32[16,128]{1,0:T(8,128)S(1)} %exponential_negate_fusion), kind=kLoop, calls=%fused_computation.33 | loop fusion | flops 12582912 | bytes 35135488 | tf_op jit(solution)/shard_map/add | solution.py:95
  364.5 8.0 broadcast.59.clone3.1
  372.5 125.3 %while.130 = (s32[]{:T(128)}, f32[32,16,128]{2,1,0:T(8,128)S(1)}, f32[32,64,16,128]{3,2,0,1:T(8,128)}, f32[32,64,16,128]{3,2,0,1:T(8,128)}, f32[32,64,16,128]{3,2,0,1:T(8,128)}, /*index=5*/s32[]{:T(128)}, s32[]{:T(128)}) while((s32[]{:T(128)}, f32[32,16,128]{2,1,0:T(8,128)S(1)}, f32[32,64,16,128]{3,2,0,1:T(8,128)}, ...), condition=%wide.region_15.16_spmd.clone, body=%wide.region_14.15_spmd.clone.sunk | while | flops 196611 | bytes 1311319 | solution.py:64
  498.6 2.3 broadcast_subtract_fusion.1
  500.9 29.8 %while.125 = (s32[]{:T(128)}, f32[32,16,128]{2,1,0:T(8,128)}, s32[]{:T(128)}, f32[16,32,16,128]{3,2,1,0:T(8,128)}, f32[16,32,16,128]{3,2,1,0:T(8,128)}, /*index=5*/s32[]{:T(128)}, s32[]{:T(128)}, s32[]{:T(128)}, s32[]{:T(128)}) while((s32[]{:T(128)}, f32[32,16,128]{2,1,0:T(8,128)}, s32[]{:T(128)}, f32[16,32,16,128]{3,2,1,0:T(8,128)}, ...), condition=%wide.region_4.5_spmd.clone, body=%wide.region_3.4_spmd.clone.sunk | while | flops 262152 | bytes 1048739 | solution.py:22
  530.6 22.9 %all-gather.23.cloned.1.call-done = f32[512,16,128]{2,1,0:T(8,128)} async-done(((f32[32,16,128]{2,1,0:T(8,128)}), f32[512,16,128]{2,1,0:T(8,128)}) %all-gather.23.cloned.1.call-update) | async-done | bytes 4194320 | tf_op jit(solution)/shard_map/all_gather | solution.py:9
  553.6 20.3 %while.131 = (s32[]{:T(128)}, f32[32,16,128]{2,1,0:T(8,128)S(1)}, s32[]{:T(128)}, f32[16,32,16,128]{3,2,1,0:T(8,128)}, f32[16,32,16,128]{3,2,1,0:T(8,128)}, /*index=5*/s32[]{:T(128)}, s32[]{:T(128)}) while((s32[]{:T(128)}, f32[32,16,128]{2,1,0:T(8,128)S(1)}, s32[]{:T(128)}, f32[16,32,16,128]{3,2,1,0:T(8,128)}, ...), condition=%wide.region_17.18_spmd.clone, body=%wide.region_16.17_spmd.clone.sunk | while | flops 262148 | bytes 1048677 | solution.py:22
  573.9 23.1 %multiply_add_fusion = (f32[32,64,16,128]{3,2,0,1:T(8,128)}, f32[32,64,16,128]{3,2,0,1:T(8,128)}) fusion(f32[32,64,16,128]{3,2,0,1:T(8,128)} %get-tuple-element.828, f32[32,16,128]{2,1,0:T(8,128)S(1)} %get-tuple-element.827, f32[32,64,128]{2,0,1:T(8,128)} %copy-done.5, f32[16,128]{1,0:T(8,128)S(1)} %exponential_negate_fusion, ...), kind=kLoop, calls=%fused_computation.32 | loop fusion | flops 25165824 | bytes 69738496 | tf_op jit(solution)/shard_map/add | solution.py:100
  597.0 7.9 broadcast.59.clone2
  604.9 111.9 %while.126 = (s32[]{:T(128)}, f32[64,16,128]{2,1,0:T(8,128)S(1)}, f32[32,64,16,128]{3,2,0,1:T(8,128)}, f32[32,64,16,128]{3,2,1,0:T(8,128)}, f32[32,64,16,128]{3,...) while((s32[]{:T(128)}, f32[64,16,128]{2,1,0:T(8,128)S(1)}, f32[32,64,16,128]{3,2,0,1:T(8,128)}, ...), condition=%wide.region_6.7_spmd.clone, body=%wide.region_5.6_spmd.clone.sunk | while | flops 655364 | bytes 3670132 | solution.py:39
  721.2 13.4 %slice.19 = f32[31,64,16,128]{3,2,0,1:T(8,128)} slice(f32[32,64,16,128]{3,2,0,1:T(8,128)} %get-tuple-element.1553), slice={[0:31], [0:64], [0:16], [0:128]} | slice | bytes 32505856 | tf_op jit(solution)/shard_map/slice | solution.py:96
  736.9 6.1 slice.18
  743.0 7.0 all-gather.19.cloned.1.call-done
  750.0 13.5 %while.127 = (s32[]{:T(128)}, f32[64,16,128]{2,1,0:T(8,128)S(1)}, s32[]{:T(128)}, f32[8,64,16,128]{3,2,1,0:T(8,128)}, f32[8,64,16,128]{3,2,1,0:T(8,128)}, /*index=5*/s32[]{:T(128)}, s32[]{:T(128)}, s32[]{:T(128)}, s32[]{:T(128)}) while((s32[]{:T(128)}, f32[64,16,128]{2,1,0:T(8,128)S(1)}, s32[]{:T(128)}, ...), condition=%wide.region_9.10_spmd.clone, body=%wide.region_8.9_spmd.clone.sunk | while | flops 524296 | bytes 2097315 | solution.py:22
  763.5 35.4 %multiply_reduce_fusion = (f32[128,16]{0,1:T(8,128)}, f32[32,64,16,128]{3,2,0,1:T(8,128)}, f32[32,64,16,128]{3,2,0,1:T(8,128)}) fusion(f32[128,32,64]{0,1,2:T(8,128)} %copy.91, f32[16,128]{1,0:T(8,128)S(1)} %exponential_negate_fusion, f32[32,64,128]{2,0,1:T(8,128)S(1)} %copy-done.7, f32[31,64,16,128]{3,2,0,1:T(8,128)} %slice.19, ...), kind=kLoop, calls=%fused_computation.28 | loop fusion | flops 50329600 | bytes 104349696 | tf_op jit(solution)/shard_map/hwnd,hwd->nd/dot_general | solution.py:123
  798.9 2.9 copy.60
  801.8 28.7 %fusion.6 = f32[32,64,1,16]{3,2,1,0:T(1,128)S(1)} fusion(f32[32,64,128,1]{2,3,1,0:T(1,128)} %bitcast.159, f32[32,64,16,128]{3,2,0,1:T(8,128)} %get-tuple-element.1097), kind=kOutput, calls=%fused_computation.29 | convolution fusion | flops 50331648 | bytes 17956864 | tf_op jit(solution)/shard_map/hwnd,hwd->hwn/dot_general | solution.py:122
  832.5 18.4 %fusion.10 = f32[32,64,1,128]{3,2,1,0:T(1,128)S(1)} fusion(f32[32,64,16,1]{2,3,1,0:T(1,128)} %copy.60, f32[32,64,16,128]{3,2,0,1:T(8,128)} %get-tuple-element.1089), kind=kOutput, calls=%fused_computation.40 | convolution fusion | flops 50331648 | bytes 17956864 | tf_op jit(solution)/shard_map/hwnd,hwn->hwd/dot_general | solution.py:116
  850.9 11.6 %all-gather.25.cloned.1.call-done = f32[2048,128]{1,0:T(8,128)} async-done(((f32[16,128]{1,0:T(8,128)}), f32[2048,128]{1,0:T(8,128)}) %all-gather.25.cloned.1.call-update) | async-done | bytes 1048592 | tf_op jit(solution)/shard_map/all_gather | solution.py:82
  864.5 10.9 %multiply_reduce_fusion.1 = f32[128,32,64]{0,1,2:T(8,128)} fusion(f32[32,64,16,128]{3,2,0,1:T(8,128)} %get-tuple-element.1088, f32[128,16]{0,1:T(8,128)S(1)} %get-tuple-element.1096), kind=kLoop, calls=%fused_computation.31 | loop fusion | flops 8126464 | bytes 17833984
  875.4 3.6 fusion.17
  879.1 28.9 %fusion.8 = f32[32,64,1,16]{3,2,1,0:T(1,128)S(1)} fusion(f32[32,64,128,1]{2,3,1,0:T(1,128)S(1)} %bitcast.158, f32[32,64,16,128]{3,2,0,1:T(8,128)} %get-tuple-element.1089), kind=kOutput, calls=%fused_computation.38 | convolution fusion | flops 50331648 | bytes 17956864 | tf_op jit(solution)/shard_map/hwnd,hwd->hwn/dot_general | solution.py:121
  (379 shorter events, 528.2 us)
Async XLA Ops:
  7.2 331.6 %all-gather.21.cloned.1.call-start = ((), (), s32[]{:S(2)}) async-start(), calls=%async_computation.4 | async-start | bytes 4718592 | tf_op jit(solution)/shard_map/all_gather | solution.py:9
  9.8 13.3 %copy-start.6 = (f32[32,64,128]{2,0,1:T(8,128)}, f32[32,64,128]{2,0,1:T(8,128)S(1)}, u32[]{:S(2)}) copy-start(f32[32,64,128]{2,0,1:T(8,128)S(1)} %copy.43) | copy-start | bytes 3145732
  23.0 5.7 copy-start
  34.9 88.0 %copy-start.3 = (f32[32,64,128]{2,1,0:T(8,128)S(1)}, f32[32,64,128]{2,1,0:T(8,128)}, u32[]{:S(2)}) copy-start(f32[32,64,128]{2,1,0:T(8,128)} %param.23) | copy-start | bytes 3145732
  34.9 95.4 %copy-start.9 = (f32[32,64,16]{1,2,0:T(8,128)S(1)}, f32[32,64,16]{1,2,0:T(8,128)}, u32[]{:S(2)}) copy-start(f32[32,64,16]{1,2,0:T(8,128)} %param.25) | copy-start | bytes 393220
  122.0 0.8 copy-start.4
  122.9 215.9 %all-gather.15.cloned.1.call-start = ((), (), s32[]{:S(2)}) async-start(), calls=%async_computation.1 | async-start | bytes 4718592 | tf_op jit(solution)/shard_map/all_gather | solution.py:9
  127.8 373.0 %all-gather.13.cloned.1.call-start = ((), (), s32[]{:S(2)}) async-start(), calls=%async_computation | async-start | bytes 4456448 | tf_op jit(solution)/shard_map/all_gather | solution.py:9
  128.5 1.0 copy-start.5
  130.3 370.6 %all-gather.17.cloned.1.call-start = ((), (), s32[]{:S(2)}) async-start(), calls=%async_computation.2 | async-start | bytes 4456448 | tf_op jit(solution)/shard_map/all_gather | solution.py:9
  335.9 0.7 copy-start.2
  336.6 216.9 %all-gather.23.cloned.1.call-start = ((), (), s32[]{:S(2)}) async-start(), calls=%async_computation.5 | async-start | bytes 4456448 | tf_op jit(solution)/shard_map/all_gather | solution.py:9
  497.8 0.7 copy-start.8
  498.5 251.5 %all-gather.19.cloned.1.call-start = ((), (), s32[]{:S(2)}) async-start(), calls=%async_computation.3 | async-start | bytes 4718592 | tf_op jit(solution)/shard_map/all_gather | solution.py:9
  716.9 0.8 copy-start.1
  717.7 144.8 %all-gather.25.cloned.1.call-start = ((), (), s32[]{:S(2)}) async-start(), calls=%async_computation.6 | async-start | bytes 1056768 | tf_op jit(solution)/shard_map/all_gather | solution.py:82
  719.6 15.0 %slice-start = ((s8[16777216]{0:T(1024)(128)(4,1)}), s8[4194304]{0:T(1024)(128)(4,1)S(1)}, s32[]{:S(2)}) async-start(s8[16777216]{0:T(1024)(128)(4,1)} %bitcast.152), calls=%async_computation.7 | async-start | bytes 8388608
  721.2 13.4 %slice-start.1 = ((s8[16777216]{0:T(1024)(128)(4,1)}), s8[4194304]{0:T(1024)(128)(4,1)S(1)}, s32[]{:S(2)}) async-start(s8[16777216]{0:T(1024)(128)(4,1)} %bitcast.152), calls=%async_computation.8 | async-start | bytes 8388608
  721.2 14.1 %slice-start.2 = ((s8[16777216]{0:T(1024)(128)(4,1)}), s8[4194304]{0:T(1024)(128)(4,1)S(1)}, s32[]{:S(2)}) async-start(s8[16777216]{0:T(1024)(128)(4,1)} %bitcast.152), calls=%async_computation.9 | async-start | bytes 8388608
  721.2 15.7 %slice-start.3 = ((s8[16777216]{0:T(1024)(128)(4,1)}), s8[4194304]{0:T(1024)(128)(4,1)S(1)}, s32[]{:S(2)}) async-start(s8[16777216]{0:T(1024)(128)(4,1)} %bitcast.152), calls=%async_computation.10 | async-start | bytes 8388608
  736.9 26.5 %copy-start.7 = (f32[32,64,128]{2,0,1:T(8,128)S(1)}, f32[32,64,128]{2,0,1:T(8,128)}, u32[]{:S(2)}) copy-start(f32[32,64,128]{2,0,1:T(8,128)} %copy-done.6) | copy-start | bytes 3145732
  830.6 33.3 %copy-start.10 = (f32[16,128]{1,0:T(8,128)S(1)}, f32[16,128]{1,0:T(8,128)}, u32[]{:S(2)}) copy-start(f32[16,128]{1,0:T(8,128)} %param.26) | copy-start | bytes 24580
Sparse Core Ops, SparseCore 0:
  123.0 35.7 all-gather.20
  160.5 32.0 all-gather.14
  195.3 51.1 all-gather.12
  336.7 54.9 all-gather.16
  498.6 54.9 all-gather.22
  717.8 32.1 all-gather.18
  799.0 63.4 all-gather.24
